TPU v7x, 32 devices: a whole 2x2x4 slice. The times are simulated.
32 devices in a mesh: rep: 2 (over x), ctx: 8 (over z, y), tp: 2 (over core).
Axes of the slice: x: 2, y: 2, z: 4, core: 2. Of those that a mesh axis runs over, the one named last changes fastest.
Arguments:
- queries: bfloat16 [4096, 4096], P(('rep', 'ctx'), 'tp'), parts along dimension 0, may hold values from -8 to 8
- rotated_key_rows: bfloat16 [4096, 512], P(('rep', 'ctx'), 'tp'), parts along dimension 0, may hold values from -8 to 8
- ordered_value_rows: bfloat16 [4096, 512], P(('rep', 'ctx'), 'tp'), parts along dimension 0, may hold values from -6 to 6
- block_order: int32 [32], P('rep'), parts along dimension 0, may hold values from 0 to 15, each once
- live_blocks: int32 [32, 12], P('rep'), parts along dimension 0, may hold values from -1 to 15, as said below
Outputs:
- attended: bfloat16 [4096, 4096], P(('rep', 'ctx', 'tp')), parts along dimension 0
- log_norm: float32 [64, 2048], P(('rep', 'tp'), 'ctx'), parts along dimension 0
There are 2 independent parts, one for each index of `rep`. A program takes and returns all parts, laid end to end along the dimension named above; each array names one. Nothing has to cross between parts.
Inputs may be any that keep to these rules, and one draw needn't show every extreme that they name: `live_blocks`: row s names block s in its first slot, then distinct blocks before s, then -1 in every unused slot; row 15 fills all 12 slots.
All inputs are finite; a program needn't handle non-finite values.
Results may differ from a plain program's by a relative error of at most 0.008.
Values may be sent and summed in bfloat16 or wider, within the bound.
A program may use at most 128 MiB of HBM per device.

v0:
```python
import jax
import jax.numpy as jnp
from jax import lax
from jax.sharding import PartitionSpec as P

HEAD_SIZE = 128
BLOCK_TOKENS = 128
NEG_LARGE = -1e30


def body(queries, rotated_key_rows, ordered_value_rows, block_order, live_blocks):
    tok_rows = queries.shape[0]
    kv_local = rotated_key_rows.shape[1] // HEAD_SIZE
    heads_local = queries.shape[1] // HEAD_SIZE
    query_groups = heads_local // kv_local
    blocks_total = block_order.shape[0]
    blocks_here = tok_rows // BLOCK_TOKENS
    factor = HEAD_SIZE ** (-0.5)
    shard_index = lax.axis_index("ctx")
    block_ids = jnp.arange(blocks_total, dtype=jnp.int32)
    my_blocks = lax.dynamic_slice_in_dim(block_order, shard_index * blocks_here, blocks_here)
    my_lists = jnp.take(live_blocks, my_blocks, axis=0)
    live_table = jnp.any(my_lists[:, :, None] == block_ids[None, None, :], axis=1)
    within = jnp.arange(BLOCK_TOKENS, dtype=jnp.int32)
    causal_square = within[None, :] <= within[:, None]
    query_heads = queries.reshape(tok_rows, kv_local, query_groups, HEAD_SIZE)
    carried = tuple(
        (
            (
                jnp.full((kv_local, query_groups, BLOCK_TOKENS), NEG_LARGE, jnp.float32),
                jnp.zeros((kv_local, query_groups, BLOCK_TOKENS), jnp.float32),
                jnp.zeros((kv_local, query_groups, BLOCK_TOKENS, HEAD_SIZE), jnp.float32),
            )
            for block_local in range(blocks_here)
        )
    )
    key_piece = lax.all_gather(rotated_key_rows, "ctx", axis=0, tiled=True)
    value_piece = lax.all_gather(ordered_value_rows, "ctx", axis=0, tiled=True)
    key_blocks = key_piece.shape[0] // BLOCK_TOKENS

    def one_key_block(turn_index, states):
        offset = turn_index * BLOCK_TOKENS
        key_part = lax.dynamic_slice_in_dim(key_piece, offset, BLOCK_TOKENS).reshape(
            BLOCK_TOKENS, kv_local, HEAD_SIZE
        )
        value_part = lax.dynamic_slice_in_dim(value_piece, offset, BLOCK_TOKENS).reshape(
            BLOCK_TOKENS, kv_local, HEAD_SIZE
        )
        key_seq = block_order[offset // BLOCK_TOKENS]
        updated = []
        for block_local in range(blocks_here):
            query_part = query_heads[block_local * BLOCK_TOKENS : (block_local + 1) * BLOCK_TOKENS]
            allowed = (key_seq != my_blocks[block_local]) | causal_square

            def compute_tile(current):
                running, denominator, weighted = current
                scores = (
                    jnp.einsum(
                        "qhgd,khd->hgqk", query_part, key_part, preferred_element_type=jnp.float32
                    )
                    * factor
                )
                scores = jnp.where(allowed, scores, NEG_LARGE)
                new_peak = jnp.maximum(running, jnp.max(scores, axis=-1))
                weights = jnp.where(allowed, jnp.exp(scores - new_peak[..., None]), 0.0)
                rescale = jnp.exp(running - new_peak)
                denominator = denominator * rescale + jnp.sum(weights, axis=-1)
                weighted = weighted * rescale[..., None] + jnp.einsum(
                    "hgqk,khd->hgqd",
                    weights.astype(jnp.bfloat16),
                    value_part,
                    preferred_element_type=jnp.float32,
                )
                return (new_peak, denominator, weighted)

            updated.append(
                lax.cond(
                    live_table[block_local, key_seq],
                    compute_tile,
                    lambda current: current,
                    states[block_local],
                )
            )
        return tuple(updated)

    states = lax.fori_loop(0, key_blocks, one_key_block, carried)
    running = jnp.concatenate([item[0] for item in states], axis=2)
    denominator = jnp.concatenate([item[1] for item in states], axis=2)
    weighted = jnp.concatenate([item[2] for item in states], axis=2)
    normed = weighted / denominator[..., None]
    merged_out = (
        jnp.transpose(normed, (2, 0, 1, 3))
        .reshape(tok_rows, heads_local * HEAD_SIZE)
        .astype(jnp.bfloat16)
    )
    log_norm = (running + jnp.log(denominator)).reshape(heads_local, tok_rows)
    attended = lax.all_to_all(merged_out, "tp", split_axis=0, concat_axis=1, tiled=True)
    return (attended, log_norm)


def solution(mesh):
    placed = (
        P(("rep", "ctx"), "tp"),
        P(("rep", "ctx"), "tp"),
        P(("rep", "ctx"), "tp"),
        P("rep"),
        P("rep", None),
    )
    return jax.shard_map(
        body,
        mesh=mesh,
        in_specs=placed,
        out_specs=(P(("rep", "ctx", "tp"), None), P(("rep", "tp"), "ctx")),
        check_vma=False,
    )
```

profile of v0, /device:TPU:0, one launch (start us, length us, event | category | flops | bytes accessed | tf_op | source)
XLA Modules:
  0.0 250.6 jit_solution(15988656583783142846)
XLA Ops:
  7.2 1.7 copy.39
  9.0 1.7 copy.40
  10.6 1.5 copy.41
  13.7 39.1 %all-gather.3.cloned.1.call-done = bf16[2048,256]{0,1:T(8,128)(2,1)} async-done(((bf16[256,256]{0,1:T(8,128)(2,1)}), bf16[2048,256]{0,1:T(8,128)(2,1)}) %all-gather.3.cloned.1.call-update) | async-done | bytes 1048592 | tf_op jit(solution)/shard_map/all_gather | solution.py:37
  52.8 40.5 %all-gather.5.cloned.1.call-done = bf16[2048,256]{0,1:T(8,128)(2,1)} async-done(((bf16[256,256]{0,1:T(8,128)(2,1)}), bf16[2048,256]{0,1:T(8,128)(2,1)}) %all-gather.5.cloned.1.call-update) | async-done | bytes 1048592 | tf_op jit(solution)/shard_map/all_gather | solution.py:38
  93.5 141.2 %while.27 = (s32[]{:T(128)}, f32[2,8,128]{2,1,0:T(8,128)S(1)}, f32[2,8,128]{2,1,0:T(8,128)S(1)}, f32[2,8,128,128]{3,2,1,0:T(8,128)S(1)}, f32[2,8,128]{2,1,0:T(8,...) while((s32[]{:T(128)}, f32[2,8,128]{2,1,0:T(8,128)S(1)}, ...), condition=%wide.region_10.11_spmd.clone.clone, body=%wide.region_1.10_spmd.clone.clone.sunk | while | flops 274260000 | bytes 12501754 | solution.py:86
  98.0 0.9 constant_dynamic-slice_fusion.7
  98.9 2.0 conditional.8
  100.2 0.7 convolution_add_fusion
  105.4 0.9 constant_dynamic-slice_fusion.7
  106.3 3.3 %conditional.9 = ((f32[2,8,128]{2,1,0:T(8,128)S(1)}, f32[2,8,128]{2,1,0:T(8,128)S(1)}, f32[2,8,128,128]{3,2,1,0:T(8,128)S(1)})) conditional(s32[]{:T(128)} %bitcast.60, (f32[2,8,128]{2,1,0:T(8,128)S(1)}, f32[2,8,128]{2,1,0:T(8,128)S(1)}, f32[2,8,128,128]{3,2,1,0:T(8,128)S(1)}) %tuple.96, (s32[2]{0:T(128)S(1)}, s32[]{:T(128)}, ...), branch_computations={%region_6.6_spmd, %region_7.9_spmd} | conditional | flops 137121792 | bytes 6111282 | solution.py:77
  108.9 0.7 convolution_add_fusion.1
  114.2 0.9 constant_dynamic-slice_fusion.7
  115.0 2.0 conditional.8
  116.3 0.7 convolution_add_fusion
  117.1 3.3 %conditional.9 = ((f32[2,8,128]{2,1,0:T(8,128)S(1)}, f32[2,8,128]{2,1,0:T(8,128)S(1)}, f32[2,8,128,128]{3,2,1,0:T(8,128)S(1)})) conditional(s32[]{:T(128)} %bitcast.60, (f32[2,8,128]{2,1,0:T(8,128)S(1)}, f32[2,8,128]{2,1,0:T(8,128)S(1)}, f32[2,8,128,128]{3,2,1,0:T(8,128)S(1)}) %tuple.96, (s32[2]{0:T(128)S(1)}, s32[]{:T(128)}, ...), branch_computations={%region_6.6_spmd, %region_7.9_spmd} | conditional | flops 137121792 | bytes 6111282 | solution.py:77
  119.6 0.7 convolution_add_fusion.1
  124.9 0.9 constant_dynamic-slice_fusion.7
  125.8 2.0 conditional.8
  127.1 0.7 convolution_add_fusion
  127.8 3.3 %conditional.9 = ((f32[2,8,128]{2,1,0:T(8,128)S(1)}, f32[2,8,128]{2,1,0:T(8,128)S(1)}, f32[2,8,128,128]{3,2,1,0:T(8,128)S(1)})) conditional(s32[]{:T(128)} %bitcast.60, (f32[2,8,128]{2,1,0:T(8,128)S(1)}, f32[2,8,128]{2,1,0:T(8,128)S(1)}, f32[2,8,128,128]{3,2,1,0:T(8,128)S(1)}) %tuple.96, (s32[2]{0:T(128)S(1)}, s32[]{:T(128)}, ...), branch_computations={%region_6.6_spmd, %region_7.9_spmd} | conditional | flops 137121792 | bytes 6111282 | solution.py:77
  130.3 0.7 convolution_add_fusion.1
  135.6 0.9 constant_dynamic-slice_fusion.7
  136.5 2.0 conditional.8
  137.8 0.7 convolution_add_fusion
  138.5 3.3 %conditional.9 = ((f32[2,8,128]{2,1,0:T(8,128)S(1)}, f32[2,8,128]{2,1,0:T(8,128)S(1)}, f32[2,8,128,128]{3,2,1,0:T(8,128)S(1)})) conditional(s32[]{:T(128)} %bitcast.60, (f32[2,8,128]{2,1,0:T(8,128)S(1)}, f32[2,8,128]{2,1,0:T(8,128)S(1)}, f32[2,8,128,128]{3,2,1,0:T(8,128)S(1)}) %tuple.96, (s32[2]{0:T(128)S(1)}, s32[]{:T(128)}, ...), branch_computations={%region_6.6_spmd, %region_7.9_spmd} | conditional | flops 137121792 | bytes 6111282 | solution.py:77
  141.1 0.7 convolution_add_fusion.1
  146.3 0.9 constant_dynamic-slice_fusion.7
  147.2 2.0 conditional.8
  148.5 0.7 convolution_add_fusion
  149.2 3.3 %conditional.9 = ((f32[2,8,128]{2,1,0:T(8,128)S(1)}, f32[2,8,128]{2,1,0:T(8,128)S(1)}, f32[2,8,128,128]{3,2,1,0:T(8,128)S(1)})) conditional(s32[]{:T(128)} %bitcast.60, (f32[2,8,128]{2,1,0:T(8,128)S(1)}, f32[2,8,128]{2,1,0:T(8,128)S(1)}, f32[2,8,128,128]{3,2,1,0:T(8,128)S(1)}) %tuple.96, (s32[2]{0:T(128)S(1)}, s32[]{:T(128)}, ...), branch_computations={%region_6.6_spmd, %region_7.9_spmd} | conditional | flops 137121792 | bytes 6111282 | solution.py:77
  151.8 0.7 convolution_add_fusion.1
  157.0 0.9 constant_dynamic-slice_fusion.7
  162.5 0.9 constant_dynamic-slice_fusion.7
  163.4 3.3 %conditional.9 = ((f32[2,8,128]{2,1,0:T(8,128)S(1)}, f32[2,8,128]{2,1,0:T(8,128)S(1)}, f32[2,8,128,128]{3,2,1,0:T(8,128)S(1)})) conditional(s32[]{:T(128)} %bitcast.60, (f32[2,8,128]{2,1,0:T(8,128)S(1)}, f32[2,8,128]{2,1,0:T(8,128)S(1)}, f32[2,8,128,128]{3,2,1,0:T(8,128)S(1)}) %tuple.96, (s32[2]{0:T(128)S(1)}, s32[]{:T(128)}, ...), branch_computations={%region_6.6_spmd, %region_7.9_spmd} | conditional | flops 137121792 | bytes 6111282 | solution.py:77
  166.0 0.7 convolution_add_fusion.1
  171.2 0.9 constant_dynamic-slice_fusion.7
  172.1 3.3 %conditional.9 = ((f32[2,8,128]{2,1,0:T(8,128)S(1)}, f32[2,8,128]{2,1,0:T(8,128)S(1)}, f32[2,8,128,128]{3,2,1,0:T(8,128)S(1)})) conditional(s32[]{:T(128)} %bitcast.60, (f32[2,8,128]{2,1,0:T(8,128)S(1)}, f32[2,8,128]{2,1,0:T(8,128)S(1)}, f32[2,8,128,128]{3,2,1,0:T(8,128)S(1)}) %tuple.96, (s32[2]{0:T(128)S(1)}, s32[]{:T(128)}, ...), branch_computations={%region_6.6_spmd, %region_7.9_spmd} | conditional | flops 137121792 | bytes 6111282 | solution.py:77
  174.7 0.7 convolution_add_fusion.1
  179.9 0.9 constant_dynamic-slice_fusion.7
  180.8 2.0 conditional.8
  182.1 0.7 convolution_add_fusion
  182.8 3.3 %conditional.9 = ((f32[2,8,128]{2,1,0:T(8,128)S(1)}, f32[2,8,128]{2,1,0:T(8,128)S(1)}, f32[2,8,128,128]{3,2,1,0:T(8,128)S(1)})) conditional(s32[]{:T(128)} %bitcast.60, (f32[2,8,128]{2,1,0:T(8,128)S(1)}, f32[2,8,128]{2,1,0:T(8,128)S(1)}, f32[2,8,128,128]{3,2,1,0:T(8,128)S(1)}) %tuple.96, (s32[2]{0:T(128)S(1)}, s32[]{:T(128)}, ...), branch_computations={%region_6.6_spmd, %region_7.9_spmd} | conditional | flops 137121792 | bytes 6111282 | solution.py:77
  185.4 0.7 convolution_add_fusion.1
  190.6 0.9 constant_dynamic-slice_fusion.7
  191.5 2.0 conditional.8
  192.8 0.7 convolution_add_fusion
  193.5 3.3 %conditional.9 = ((f32[2,8,128]{2,1,0:T(8,128)S(1)}, f32[2,8,128]{2,1,0:T(8,128)S(1)}, f32[2,8,128,128]{3,2,1,0:T(8,128)S(1)})) conditional(s32[]{:T(128)} %bitcast.60, (f32[2,8,128]{2,1,0:T(8,128)S(1)}, f32[2,8,128]{2,1,0:T(8,128)S(1)}, f32[2,8,128,128]{3,2,1,0:T(8,128)S(1)}) %tuple.96, (s32[2]{0:T(128)S(1)}, s32[]{:T(128)}, ...), branch_computations={%region_6.6_spmd, %region_7.9_spmd} | conditional | flops 137121792 | bytes 6111282 | solution.py:77
  196.1 0.7 convolution_add_fusion.1
  201.4 0.9 constant_dynamic-slice_fusion.7
  206.8 0.9 constant_dynamic-slice_fusion.7
  207.7 3.3 %conditional.9 = ((f32[2,8,128]{2,1,0:T(8,128)S(1)}, f32[2,8,128]{2,1,0:T(8,128)S(1)}, f32[2,8,128,128]{3,2,1,0:T(8,128)S(1)})) conditional(s32[]{:T(128)} %bitcast.60, (f32[2,8,128]{2,1,0:T(8,128)S(1)}, f32[2,8,128]{2,1,0:T(8,128)S(1)}, f32[2,8,128,128]{3,2,1,0:T(8,128)S(1)}) %tuple.96, (s32[2]{0:T(128)S(1)}, s32[]{:T(128)}, ...), branch_computations={%region_6.6_spmd, %region_7.9_spmd} | conditional | flops 137121792 | bytes 6111282 | solution.py:77
  215.6 0.9 constant_dynamic-slice_fusion.7
  221.0 0.9 constant_dynamic-slice_fusion.7
  221.9 2.0 conditional.8
  223.2 0.7 convolution_add_fusion
  228.5 0.9 constant_dynamic-slice_fusion.7
  229.4 2.0 conditional.8
  230.7 0.7 convolution_add_fusion
  231.4 3.3 %conditional.9 = ((f32[2,8,128]{2,1,0:T(8,128)S(1)}, f32[2,8,128]{2,1,0:T(8,128)S(1)}, f32[2,8,128,128]{3,2,1,0:T(8,128)S(1)})) conditional(s32[]{:T(128)} %bitcast.60, (f32[2,8,128]{2,1,0:T(8,128)S(1)}, f32[2,8,128]{2,1,0:T(8,128)S(1)}, f32[2,8,128,128]{3,2,1,0:T(8,128)S(1)}) %tuple.96, (s32[2]{0:T(128)S(1)}, s32[]{:T(128)}, ...), branch_computations={%region_6.6_spmd, %region_7.9_spmd} | conditional | flops 137121792 | bytes 6111282 | solution.py:77
  233.9 0.7 convolution_add_fusion.1
  234.7 0.7 fusion.27
  236.6 4.6 %all_to_all.16 = bf16[2,128,2048]{2,1,0:T(8,128)(2,1)S(1)} all-to-all(bf16[2,128,2048]{2,1,0:T(8,128)(2,1)S(1)} %convert_element_type.44), channel_id=1, replica_groups=mesh['rep'=2,'ctx'=8,'tp'=2] {'tp'}, dimensions={0} | all-to-all | bytes 2097152 | tf_op jit(solution)/shard_map/all_to_all | solution.py:97
  241.8 1.3 copy.45
  (218 shorter events, 44.4 us)
Async XLA Ops:
  7.2 5.8 %copy-start = (s32[16,12]{1,0:T(8,128)S(1)}, s32[16,12]{1,0:T(8,128)}, u32[]{:S(2)}) copy-start(s32[16,12]{1,0:T(8,128)} %param.15) | copy-start | bytes 2308
  7.2 45.6 %all-gather.3.cloned.1.call-start = ((), (), s32[]{:S(2)}) async-start(), calls=%async_computation.1 | async-start | bytes 1179648 | tf_op jit(solution)/shard_map/all_gather | solution.py:37
  8.9 84.3 %all-gather.5.cloned.1.call-start = ((), (), s32[]{:S(2)}) async-start(), calls=%async_computation.2 | async-start | bytes 1179648 | tf_op jit(solution)/shard_map/all_gather | solution.py:38
  12.1 0.7 copy-start.1
Sparse Core Ops, SparseCore 0:
  10.6 42.1 all-gather.2
  54.8 38.3 all-gather.4
where the time goes:
time: 253 us; the launch traced here: 251 us
  waiting for transfers between devices  79.6 us (31%)
  loops' own time  74.1 us (29%)
  local copies, waits for them, and re-layouts  50.8 us (20%)
  matrix products  21 us (8%)
  between operations  14.2 us (6%)
  other arithmetic  6.35 us (3%)
  blocking collectives  4.58 us (2%)
    another operation x1, loops' own time, body(): states = lax.fori_loop(0, key_blocks, one_key_block, carried)  52.4 us
    all_gather x1, waiting for transfers between devices, body(): value_piece = lax.all_gather(ordered_value_rows, 'ctx', axis=0, tiled=True)  40.5 us
    all_gather x1, waiting for transfers between devices, body(): key_piece = lax.all_gather(rotated_key_rows, 'ctx', axis=0, tiled=True)  39.1 us
    another operation x32, loops' own time, one_key_block(): lax.cond(live_table[block_local, key_seq], compute_tile, lambda current:...  21.7 us
    dynamic_slice x16, local copies, waits for them, and re-layouts, one_key_block(): lax.dynamic_slice_in_dim(value_piece, offset, BLOCK_TOKENS)  14.3 us
    dot_general x20, matrix products, compute_tile(): jnp.einsum('hgqk,khd->hgqd', weights.astype(jnp.bfloat16), value_part, pr...  13.7 us
    dynamic_slice x16, local copies, waits for them, and re-layouts, one_key_block(): live_table[block_local, key_seq]  10.6 us
    dynamic_slice x16, local copies, waits for them, and re-layouts, one_key_block(): key_seq = block_order[offset // BLOCK_TOKENS]  9.39 us
  transfers between devices with their start and end apart: 2, of which 2 were waited for; matrix products, arithmetic and copies ran while one was open for 2% of the time, Pallas kernels for 0%

commit v1 on v0

--- a/solution.py
+++ b/solution.py
@@ -34,7 +34,12 @@
             for block_local in range(blocks_here)
         )
     )
-    key_piece = lax.all_gather(rotated_key_rows, "ctx", axis=0, tiled=True)
+    ring = [rotated_key_rows]
+    for hop in range(7):
+        ring.append(lax.ppermute(ring[-1], "ctx", [(dev, (dev + 1) % 8) for dev in range(8)]))
+    key_piece = jnp.roll(
+        jnp.concatenate(ring[::-1], axis=0), (lax.axis_index("ctx") + 1) * ring[0].shape[0], axis=0
+    )
     value_piece = lax.all_gather(ordered_value_rows, "ctx", axis=0, tiled=True)
     key_blocks = key_piece.shape[0] // BLOCK_TOKENS
 

time: 253 us -> 240 us (0.949)
  waiting for transfers between devices: 79.6 us -> 67.2 us
  loops' own time: 74.1 us -> 69.4 us
  starting transfers between devices: 0.08 us -> 3.1 us
    ppermute x0 -> x7, waiting for transfers between devices: none -> 49.1 us  [body(): lax.ppermute(ring[-1], 'ctx', [(dev, (dev + 1) % 8) for dev in range(8)])]
    all_gather x1 -> x0, waiting for transfers between devices: 39.1 us -> none  [body(): key_piece = lax.all_gather(rotated_key_rows, 'ctx', axis=0, tiled=True)]
    all_gather x1, waiting for transfers between devices: 40.5 us -> 18.1 us  [body(): value_piece = lax.all_gather(ordered_value_rows, 'ctx', axis=0, tiled=True)]
    another operation x1, loops' own time: 52.4 us -> 48.8 us  [body(): states = lax.fori_loop(0, key_blocks, one_key_block, carried)]
    ppermute x0 -> x7, starting transfers between devices: none -> 3.06 us  [body(): lax.ppermute(ring[-1], 'ctx', [(dev, (dev + 1) % 8) for dev in range(8)])]
    unnamed x9 -> x24, local copies, waits for them, and re-layouts: 6.79 us -> 6.28 us
  transfers between devices with their start and end apart: 2 -> 8, of which waited for: 2 -> 8; matrix products, arithmetic and copies ran while one was open for 2% -> 3% of each run, Pallas kernels for 0% -> 0%
where the time goes in v1:
time: 240 us; the launch traced here: 238 us
  loops' own time  69.4 us (29%)
  waiting for transfers between devices  67.2 us (28%)
  local copies, waits for them, and re-layouts  51.3 us (21%)
  matrix products  21 us (9%)
  between operations  14.3 us (6%)
  other arithmetic  6.99 us (3%)
  blocking collectives  4.58 us (2%)
  starting transfers between devices  3.1 us (1%)
    ppermute x7, waiting for transfers between devices, body(): lax.ppermute(ring[-1], 'ctx', [(dev, (dev + 1) % 8) for dev in range(8)])  49.1 us
    another operation x1, loops' own time, body(): states = lax.fori_loop(0, key_blocks, one_key_block, carried)  48.8 us
    another operation x32, loops' own time, one_key_block(): lax.cond(live_table[block_local, key_seq], compute_tile, lambda current:...  20.6 us
    all_gather x1, waiting for transfers between devices, body(): value_piece = lax.all_gather(ordered_value_rows, 'ctx', axis=0, tiled=True)  18.1 us
    dynamic_slice x16, local copies, waits for them, and re-layouts, one_key_block(): lax.dynamic_slice_in_dim(value_piece, offset, BLOCK_TOKENS)  14.2 us
    dot_general x20, matrix products, compute_tile(): jnp.einsum('hgqk,khd->hgqd', weights.astype(jnp.bfloat16), value_part, pr...  13.7 us
    dynamic_slice x16, local copies, waits for them, and re-layouts, one_key_block(): live_table[block_local, key_seq]  10.6 us
    dynamic_slice x16, local copies, waits for them, and re-layouts, one_key_block(): key_seq = block_order[offset // BLOCK_TOKENS]  9.25 us
  transfers between devices with their start and end apart: 8, of which 8 were waited for; matrix products, arithmetic and copies ran while one was open for 3% of the time, Pallas kernels for 0%

profile of v1, /device:TPU:0, one launch (start us, length us, event | category | flops | bytes accessed | tf_op | source)
XLA Modules:
  0.0 237.9 jit_solution(8729510954161521761)
XLA Ops:
  7.2 1.0 copy.43
  8.2 3.0 %collective-permute-start = (bf16[256,256]{0,1:T(8,128)(2,1)S(1)}, bf16[256,256]{0,1:T(8,128)(2,1)S(1)}, u32[]{:S(2)}, u32[]{:S(2)}) collective-permute-start(bf16[256,256]{0,1:T(8,128)(2,1)S(1)} %copy.43), channel_id=1, source_target_pairs={{0,2},{2,4},{4,6},{6,8},{8,10},{10,12},{12,14},{14,0},{1,3},{3,5},... | collective-permute-start | bytes 393224 | tf_op jit(solution)/shard_map/ppermute | solution.py:39
  11.3 6.5 %collective-permute-done = bf16[256,256]{0,1:T(8,128)(2,1)S(1)} collective-permute-done((bf16[256,256]{0,1:T(8,128)(2,1)S(1)}, bf16[256,256]{0,1:T(8,128)(2,1)S(1)}, u32[]{:S(2)}, u32[]{:S(2)}) %collective-permute-start) | collective-permute-done | bytes 131104 | tf_op jit(solution)/shard_map/ppermute | solution.py:39
  17.8 7.7 %collective-permute-done.1 = bf16[256,256]{0,1:T(8,128)(2,1)S(1)} collective-permute-done((bf16[256,256]{0,1:T(8,128)(2,1)S(1)}, bf16[256,256]{0,1:T(8,128)(2,1)S(1)}, u32[]{:S(2)}, u32[]{:S(2)}) %collective-permute-start.1) | collective-permute-done | bytes 131104 | tf_op jit(solution)/shard_map/ppermute | solution.py:39
  25.5 7.7 %collective-permute-done.2 = bf16[256,256]{0,1:T(8,128)(2,1)S(1)} collective-permute-done((bf16[256,256]{0,1:T(8,128)(2,1)S(1)}, bf16[256,256]{0,1:T(8,128)(2,1)S(1)}, u32[]{:S(2)}, u32[]{:S(2)}) %collective-permute-start.2) | collective-permute-done | bytes 131104 | tf_op jit(solution)/shard_map/ppermute | solution.py:39
  33.2 7.7 %collective-permute-done.3 = bf16[256,256]{0,1:T(8,128)(2,1)S(1)} collective-permute-done((bf16[256,256]{0,1:T(8,128)(2,1)S(1)}, bf16[256,256]{0,1:T(8,128)(2,1)S(1)}, u32[]{:S(2)}, u32[]{:S(2)}) %collective-permute-start.3) | collective-permute-done | bytes 131104 | tf_op jit(solution)/shard_map/ppermute | solution.py:39
  40.8 1.6 copy.46
  42.5 0.7 compare_and_fusion
  43.2 5.3 %collective-permute-done.4 = bf16[256,256]{0,1:T(8,128)(2,1)S(1)} collective-permute-done((bf16[256,256]{0,1:T(8,128)(2,1)S(1)}, bf16[256,256]{0,1:T(8,128)(2,1)S(1)}, u32[]{:S(2)}, u32[]{:S(2)}) %collective-permute-start.4) | collective-permute-done | bytes 131104 | tf_op jit(solution)/shard_map/ppermute | solution.py:39
  49.1 8.5 %collective-permute-done.5 = bf16[256,256]{0,1:T(8,128)(2,1)S(1)} collective-permute-done((bf16[256,256]{0,1:T(8,128)(2,1)S(1)}, bf16[256,256]{0,1:T(8,128)(2,1)S(1)}, u32[]{:S(2)}, u32[]{:S(2)}) %collective-permute-start.5) | collective-permute-done | bytes 131104 | tf_op jit(solution)/shard_map/ppermute | solution.py:39
  57.6 1.5 copy.47
  59.9 5.8 %collective-permute-done.6 = bf16[256,256]{0,1:T(8,128)(2,1)S(1)} collective-permute-done((bf16[256,256]{0,1:T(8,128)(2,1)S(1)}, bf16[256,256]{0,1:T(8,128)(2,1)S(1)}, u32[]{:S(2)}, u32[]{:S(2)}) %collective-permute-start.6) | collective-permute-done | bytes 131104 | tf_op jit(solution)/shard_map/ppermute | solution.py:39
  66.0 1.0 constant_dynamic-slice_fusion.4
  67.1 18.1 %all-gather.2.cloned.1.call-done = bf16[2048,256]{0,1:T(8,128)(2,1)} async-done(((bf16[256,256]{0,1:T(8,128)(2,1)}), bf16[2048,256]{0,1:T(8,128)(2,1)}) %all-gather.2.cloned.1.call-update) | async-done | bytes 1048592 | tf_op jit(solution)/shard_map/all_gather | solution.py:43
  85.4 136.5 %while.27 = (s32[]{:T(128)}, f32[2,8,128]{2,1,0:T(8,128)S(1)}, f32[2,8,128]{2,1,0:T(8,128)S(1)}, f32[2,8,128,128]{3,2,1,0:T(8,128)S(1)}, f32[2,8,128]{2,1,0:T(8,...) while((s32[]{:T(128)}, f32[2,8,128]{2,1,0:T(8,128)S(1)}, ...), condition=%wide.region_10.11_spmd.clone.clone, body=%wide.region_1.10_spmd.clone.clone.sunk | while | flops 274260000 | bytes 12501762 | solution.py:91
  89.0 0.9 constant_dynamic-slice_fusion.8
  89.9 1.9 conditional.8
  91.1 0.7 convolution_add_fusion
  96.1 0.9 constant_dynamic-slice_fusion.8
  97.7 3.3 %conditional.9 = ((f32[2,8,128]{2,1,0:T(8,128)S(1)}, f32[2,8,128]{2,1,0:T(8,128)S(1)}, f32[2,8,128,128]{3,2,1,0:T(8,128)S(1)})) conditional(s32[]{:T(128)} %bitcast.60, (f32[2,8,128]{2,1,0:T(8,128)S(1)}, f32[2,8,128]{2,1,0:T(8,128)S(1)}, f32[2,8,128,128]{3,2,1,0:T(8,128)S(1)}) %tuple.96, (s32[2]{0:T(128)S(1)}, s32[]{:T(128)}, ...), branch_computations={%region_6.6_spmd, %region_7.9_spmd} | conditional | flops 137121792 | bytes 6111282 | solution.py:82
  100.3 0.7 convolution_add_fusion.1
  104.6 0.9 constant_dynamic-slice_fusion.8
  105.5 1.9 conditional.8
  106.7 0.7 convolution_add_fusion
  108.1 3.3 %conditional.9 = ((f32[2,8,128]{2,1,0:T(8,128)S(1)}, f32[2,8,128]{2,1,0:T(8,128)S(1)}, f32[2,8,128,128]{3,2,1,0:T(8,128)S(1)})) conditional(s32[]{:T(128)} %bitcast.60, (f32[2,8,128]{2,1,0:T(8,128)S(1)}, f32[2,8,128]{2,1,0:T(8,128)S(1)}, f32[2,8,128,128]{3,2,1,0:T(8,128)S(1)}) %tuple.96, (s32[2]{0:T(128)S(1)}, s32[]{:T(128)}, ...), branch_computations={%region_6.6_spmd, %region_7.9_spmd} | conditional | flops 137121792 | bytes 6111282 | solution.py:82
  115.0 0.9 constant_dynamic-slice_fusion.8
  115.9 1.9 conditional.8
  117.1 0.7 convolution_add_fusion
  118.5 3.3 %conditional.9 = ((f32[2,8,128]{2,1,0:T(8,128)S(1)}, f32[2,8,128]{2,1,0:T(8,128)S(1)}, f32[2,8,128,128]{3,2,1,0:T(8,128)S(1)})) conditional(s32[]{:T(128)} %bitcast.60, (f32[2,8,128]{2,1,0:T(8,128)S(1)}, f32[2,8,128]{2,1,0:T(8,128)S(1)}, f32[2,8,128,128]{3,2,1,0:T(8,128)S(1)}) %tuple.96, (s32[2]{0:T(128)S(1)}, s32[]{:T(128)}, ...), branch_computations={%region_6.6_spmd, %region_7.9_spmd} | conditional | flops 137121792 | bytes 6111282 | solution.py:82
  125.4 0.9 constant_dynamic-slice_fusion.8
  126.2 1.9 conditional.8
  127.5 0.7 convolution_add_fusion
  128.8 3.3 %conditional.9 = ((f32[2,8,128]{2,1,0:T(8,128)S(1)}, f32[2,8,128]{2,1,0:T(8,128)S(1)}, f32[2,8,128,128]{3,2,1,0:T(8,128)S(1)})) conditional(s32[]{:T(128)} %bitcast.60, (f32[2,8,128]{2,1,0:T(8,128)S(1)}, f32[2,8,128]{2,1,0:T(8,128)S(1)}, f32[2,8,128,128]{3,2,1,0:T(8,128)S(1)}) %tuple.96, (s32[2]{0:T(128)S(1)}, s32[]{:T(128)}, ...), branch_computations={%region_6.6_spmd, %region_7.9_spmd} | conditional | flops 137121792 | bytes 6111282 | solution.py:82
  131.4 0.7 convolution_add_fusion.1
  135.7 0.9 constant_dynamic-slice_fusion.8
  136.6 1.9 conditional.8
  139.2 3.3 %conditional.9 = ((f32[2,8,128]{2,1,0:T(8,128)S(1)}, f32[2,8,128]{2,1,0:T(8,128)S(1)}, f32[2,8,128,128]{3,2,1,0:T(8,128)S(1)})) conditional(s32[]{:T(128)} %bitcast.60, (f32[2,8,128]{2,1,0:T(8,128)S(1)}, f32[2,8,128]{2,1,0:T(8,128)S(1)}, f32[2,8,128,128]{3,2,1,0:T(8,128)S(1)}) %tuple.96, (s32[2]{0:T(128)S(1)}, s32[]{:T(128)}, ...), branch_computations={%region_6.6_spmd, %region_7.9_spmd} | conditional | flops 137121792 | bytes 6111282 | solution.py:82
  146.1 0.9 constant_dynamic-slice_fusion.8
  151.3 0.9 constant_dynamic-slice_fusion.8
  152.9 3.3 %conditional.9 = ((f32[2,8,128]{2,1,0:T(8,128)S(1)}, f32[2,8,128]{2,1,0:T(8,128)S(1)}, f32[2,8,128,128]{3,2,1,0:T(8,128)S(1)})) conditional(s32[]{:T(128)} %bitcast.60, (f32[2,8,128]{2,1,0:T(8,128)S(1)}, f32[2,8,128]{2,1,0:T(8,128)S(1)}, f32[2,8,128,128]{3,2,1,0:T(8,128)S(1)}) %tuple.96, (s32[2]{0:T(128)S(1)}, s32[]{:T(128)}, ...), branch_computations={%region_6.6_spmd, %region_7.9_spmd} | conditional | flops 137121792 | bytes 6111282 | solution.py:82
  159.8 0.9 constant_dynamic-slice_fusion.8
  161.4 3.3 %conditional.9 = ((f32[2,8,128]{2,1,0:T(8,128)S(1)}, f32[2,8,128]{2,1,0:T(8,128)S(1)}, f32[2,8,128,128]{3,2,1,0:T(8,128)S(1)})) conditional(s32[]{:T(128)} %bitcast.60, (f32[2,8,128]{2,1,0:T(8,128)S(1)}, f32[2,8,128]{2,1,0:T(8,128)S(1)}, f32[2,8,128,128]{3,2,1,0:T(8,128)S(1)}) %tuple.96, (s32[2]{0:T(128)S(1)}, s32[]{:T(128)}, ...), branch_computations={%region_6.6_spmd, %region_7.9_spmd} | conditional | flops 137121792 | bytes 6111282 | solution.py:82
  164.0 0.7 convolution_add_fusion.1
  168.3 0.9 constant_dynamic-slice_fusion.8
  169.2 1.9 conditional.8
  170.4 0.7 convolution_add_fusion
  171.8 3.3 %conditional.9 = ((f32[2,8,128]{2,1,0:T(8,128)S(1)}, f32[2,8,128]{2,1,0:T(8,128)S(1)}, f32[2,8,128,128]{3,2,1,0:T(8,128)S(1)})) conditional(s32[]{:T(128)} %bitcast.60, (f32[2,8,128]{2,1,0:T(8,128)S(1)}, f32[2,8,128]{2,1,0:T(8,128)S(1)}, f32[2,8,128,128]{3,2,1,0:T(8,128)S(1)}) %tuple.96, (s32[2]{0:T(128)S(1)}, s32[]{:T(128)}, ...), branch_computations={%region_6.6_spmd, %region_7.9_spmd} | conditional | flops 137121792 | bytes 6111282 | solution.py:82
  174.4 0.7 convolution_add_fusion.1
  178.7 0.9 constant_dynamic-slice_fusion.8
  179.6 1.9 conditional.8
  182.2 3.3 %conditional.9 = ((f32[2,8,128]{2,1,0:T(8,128)S(1)}, f32[2,8,128]{2,1,0:T(8,128)S(1)}, f32[2,8,128,128]{3,2,1,0:T(8,128)S(1)})) conditional(s32[]{:T(128)} %bitcast.60, (f32[2,8,128]{2,1,0:T(8,128)S(1)}, f32[2,8,128]{2,1,0:T(8,128)S(1)}, f32[2,8,128,128]{3,2,1,0:T(8,128)S(1)}) %tuple.96, (s32[2]{0:T(128)S(1)}, s32[]{:T(128)}, ...), branch_computations={%region_6.6_spmd, %region_7.9_spmd} | conditional | flops 137121792 | bytes 6111282 | solution.py:82
  184.7 0.7 convolution_add_fusion.1
  189.0 0.9 constant_dynamic-slice_fusion.8
  194.3 0.9 constant_dynamic-slice_fusion.8
  195.9 3.3 %conditional.9 = ((f32[2,8,128]{2,1,0:T(8,128)S(1)}, f32[2,8,128]{2,1,0:T(8,128)S(1)}, f32[2,8,128,128]{3,2,1,0:T(8,128)S(1)})) conditional(s32[]{:T(128)} %bitcast.60, (f32[2,8,128]{2,1,0:T(8,128)S(1)}, f32[2,8,128]{2,1,0:T(8,128)S(1)}, f32[2,8,128,128]{3,2,1,0:T(8,128)S(1)}) %tuple.96, (s32[2]{0:T(128)S(1)}, s32[]{:T(128)}, ...), branch_computations={%region_6.6_spmd, %region_7.9_spmd} | conditional | flops 137121792 | bytes 6111282 | solution.py:82
  202.8 0.9 constant_dynamic-slice_fusion.8
  208.0 0.9 constant_dynamic-slice_fusion.8
  208.9 1.9 conditional.8
  215.1 0.9 constant_dynamic-slice_fusion.8
  216.0 1.9 conditional.8
  218.6 3.3 %conditional.9 = ((f32[2,8,128]{2,1,0:T(8,128)S(1)}, f32[2,8,128]{2,1,0:T(8,128)S(1)}, f32[2,8,128,128]{3,2,1,0:T(8,128)S(1)})) conditional(s32[]{:T(128)} %bitcast.60, (f32[2,8,128]{2,1,0:T(8,128)S(1)}, f32[2,8,128]{2,1,0:T(8,128)S(1)}, f32[2,8,128,128]{3,2,1,0:T(8,128)S(1)}) %tuple.96, (s32[2]{0:T(128)S(1)}, s32[]{:T(128)}, ...), branch_computations={%region_6.6_spmd, %region_7.9_spmd} | conditional | flops 137121792 | bytes 6111282 | solution.py:82
  221.9 0.7 fusion.27
  223.8 4.6 %all_to_all.16 = bf16[2,128,2048]{2,1,0:T(8,128)(2,1)S(1)} all-to-all(bf16[2,128,2048]{2,1,0:T(8,128)(2,1)S(1)} %convert_element_type.44), channel_id=1, replica_groups=mesh['rep'=2,'ctx'=8,'tp'=2] {'tp'}, dimensions={0} | all-to-all | bytes 2097152 | tf_op jit(solution)/shard_map/all_to_all | solution.py:102
  229.1 1.3 copy.51
  (246 shorter events, 50.6 us)
Async XLA Ops:
  7.2 41.4 %copy-start = (s32[16,12]{1,0:T(8,128)S(1)}, s32[16,12]{1,0:T(8,128)}, u32[]{:S(2)}) copy-start(s32[16,12]{1,0:T(8,128)} %param.15) | copy-start | bytes 2308
  7.2 78.0 %all-gather.2.cloned.1.call-start = ((), (), s32[]{:S(2)}) async-start(), calls=%async_computation.1 | async-start | bytes 1179648 | tf_op jit(solution)/shard_map/all_gather | solution.py:43
  8.2 9.6 %collective-permute-start = (bf16[256,256]{0,1:T(8,128)(2,1)S(1)}, bf16[256,256]{0,1:T(8,128)(2,1)S(1)}, u32[]{:S(2)}, u32[]{:S(2)}) collective-permute-start(bf16[256,256]{0,1:T(8,128)(2,1)S(1)} %copy.43), channel_id=1, source_target_pairs={{0,2},{2,4},{4,6},{6,8},{8,10},{10,12},{12,14},{14,0},{1,3},{3,5},... | collective-permute-start | bytes 393224 | tf_op jit(solution)/shard_map/ppermute | solution.py:39
  17.8 7.7 %collective-permute-start.1 = (bf16[256,256]{0,1:T(8,128)(2,1)S(1)}, bf16[256,256]{0,1:T(8,128)(2,1)S(1)}, u32[]{:S(2)}, u32[]{:S(2)}) collective-permute-start(bf16[256,256]{0,1:T(8,128)(2,1)S(1)} %collective-permute-done), channel_id=1, source_target_pairs={{0,2},{2,4},{4,6},{6,8},{8,10},{10,12},{12,14},{14,0},{1,3},{3,5},... | collective-permute-start | bytes 393224 | tf_op jit(solution)/shard_map/ppermute | solution.py:39
  25.5 7.7 %collective-permute-start.2 = (bf16[256,256]{0,1:T(8,128)(2,1)S(1)}, bf16[256,256]{0,1:T(8,128)(2,1)S(1)}, u32[]{:S(2)}, u32[]{:S(2)}) collective-permute-start(bf16[256,256]{0,1:T(8,128)(2,1)S(1)} %collective-permute-done.1), channel_id=1, source_target_pairs={{0,2},{2,4},{4,6},{6,8},{8,10},{10,12},{12,14},{14,0},{1,3},{3,5},... | collective-permute-start | bytes 393224 | tf_op jit(solution)/shard_map/ppermute | solution.py:39
  33.1 7.7 %collective-permute-start.3 = (bf16[256,256]{0,1:T(8,128)(2,1)S(1)}, bf16[256,256]{0,1:T(8,128)(2,1)S(1)}, u32[]{:S(2)}, u32[]{:S(2)}) collective-permute-start(bf16[256,256]{0,1:T(8,128)(2,1)S(1)} %collective-permute-done.2), channel_id=1, source_target_pairs={{0,2},{2,4},{4,6},{6,8},{8,10},{10,12},{12,14},{14,0},{1,3},{3,5},... | collective-permute-start | bytes 393224 | tf_op jit(solution)/shard_map/ppermute | solution.py:39
  40.8 7.7 %collective-permute-start.4 = (bf16[256,256]{0,1:T(8,128)(2,1)S(1)}, bf16[256,256]{0,1:T(8,128)(2,1)S(1)}, u32[]{:S(2)}, u32[]{:S(2)}) collective-permute-start(bf16[256,256]{0,1:T(8,128)(2,1)S(1)} %collective-permute-done.3), channel_id=1, source_target_pairs={{0,2},{2,4},{4,6},{6,8},{8,10},{10,12},{12,14},{14,0},{1,3},{3,5},... | collective-permute-start | bytes 393224 | tf_op jit(solution)/shard_map/ppermute | solution.py:39
  48.5 9.0 %collective-permute-start.5 = (bf16[256,256]{0,1:T(8,128)(2,1)S(1)}, bf16[256,256]{0,1:T(8,128)(2,1)S(1)}, u32[]{:S(2)}, u32[]{:S(2)}) collective-permute-start(bf16[256,256]{0,1:T(8,128)(2,1)S(1)} %collective-permute-done.4), channel_id=1, source_target_pairs={{0,2},{2,4},{4,6},{6,8},{8,10},{10,12},{12,14},{14,0},{1,3},{3,5},... | collective-permute-start | bytes 393224 | tf_op jit(solution)/shard_map/ppermute | solution.py:39
  57.6 8.2 %collective-permute-start.6 = (bf16[256,256]{0,1:T(8,128)(2,1)S(1)}, bf16[256,256]{0,1:T(8,128)(2,1)S(1)}, u32[]{:S(2)}, u32[]{:S(2)}) collective-permute-start(bf16[256,256]{0,1:T(8,128)(2,1)S(1)} %collective-permute-done.5), channel_id=1, source_target_pairs={{0,2},{2,4},{4,6},{6,8},{8,10},{10,12},{12,14},{14,0},{1,3},{3,5},... | collective-permute-start | bytes 393224 | tf_op jit(solution)/shard_map/ppermute | solution.py:39
  66.0 19.3 %copy-start.1 = (s32[16]{0:T(128)S(1)}, s32[16]{0:T(128)}, u32[]{:S(2)}) copy-start(s32[16]{0:T(128)} %param.14) | copy-start | bytes 196
Sparse Core Ops, SparseCore 0:
  42.6 42.4 all-gather.1
